TPU v7x, 32 devices: a whole 2x2x4 slice. The times are simulated.
32 devices in a mesh: rep: 4 (over y, x), shard: 8 (over z, core).
Axes of the slice: x: 2, y: 2, z: 4, core: 2. Of those that a mesh axis runs over, the one named last changes fastest.
Arguments:
- tokens: bfloat16 [8192, 1024], P(('rep', 'shard')), may hold values from -6 to 6
- cotangent: bfloat16 [8192, 1024], P(('rep', 'shard')), may hold values from -6 to 6
- positions: int32 [8192], P(('rep', 'shard')), may hold values from 0 to 255, as said below
- counts: int32 [32], P(('rep', 'shard')), may hold values from 128 to 256, as said below
- attn_weight: bfloat16 [1024, 3072], P('shard'), may hold values from -0.75 to 0.75
- ffn_weight: bfloat16 [4608, 3, 1024], P('shard'), may hold values from -0.1875 to 0.1875
- gains: bfloat16 [2, 1024], P(None, 'shard'), may hold values from 0.099609375 to 1.8984375
- qk_gains: bfloat16 [2, 64], P(None, 'shard'), as said below
Outputs:
- output: bfloat16 [8192, 1024], P(('rep', 'shard'))
- grad_input: bfloat16 [8192, 1024], P(('rep', 'shard'))
- grad_attn: float32 [1024, 3072], P('shard')
- grad_ffn: float32 [4608, 3, 1024], P('shard')
- grad_gains: float32 [2, 1024], P(None, 'shard')
- grad_qk: float32 [2, 64], P(None, 'shard')
Inputs may be any that keep to these rules, and one draw needn't show every extreme that they name: `counts`: one device holds 256 real tokens and another 128 in every draw. `positions`: sequences lie whole inside one device's block of 256 slots, one after another; slots at or past the block's count hold 0. `qk_gains`: positive scales.
All inputs are finite; a program needn't handle non-finite values.
Results may differ from a plain program's by a relative error of at most 0.018.
Values may be sent and summed in bfloat16 or wider, within the bound.
A program may use at most 320 MiB of HBM per device.

v0:
```python
import jax
import jax.numpy as jnp
from jax import lax
from jax.sharding import PartitionSpec as P

QUERY_HEADS = 16
KEY_VALUE_HEADS = 8
HEAD_WIDTH = 64
QUERY_FEATURES = 1024
KEY_FEATURES = 512


EPS = 1e-05
THETA = 1000000.0


def rope_tables(positions, head_size):
    half = head_size // 2
    freq = THETA ** (-2.0 * jnp.arange(half, dtype=jnp.float32) / head_size)
    angle = positions.astype(jnp.float32)[:, None] * freq[None, :]
    return (jnp.cos(angle), jnp.sin(angle))


def apply_rotation(vectors, cosine_table, sine_table, sign):
    half = vectors.shape[-1] // 2
    upper = vectors[..., :half]
    lower = vectors[..., half:]
    cos_b = cosine_table[:, None, :]
    sin_b = sine_table[:, None, :] * sign
    return jnp.concatenate([upper * cos_b - lower * sin_b, lower * cos_b + upper * sin_b], axis=-1)


def rms_back(grad_normed, unit, inverse, gain):
    inner = grad_normed * gain
    return inverse * (inner - unit * jnp.mean(inner * unit, axis=-1, keepdims=True))


def times_trans(left, right):
    return lax.dot_general(
        left, right, (((1,), (1,)), ((), ())), preferred_element_type=jnp.float32
    )


def trans_times(left, right):
    return lax.dot_general(
        left, right, (((0,), (0,)), ((), ())), preferred_element_type=jnp.float32
    )


def local(tokens, cotangent, positions, counts, attn_weight, ffn_weight, gains, qk_gains):
    token_rows = tokens.shape[0]
    width = QUERY_FEATURES + 2 * KEY_FEATURES
    replica_group = QUERY_HEADS // KEY_VALUE_HEADS
    scale = HEAD_WIDTH ** (-0.5)
    full_attn, full_gains, full_qk = (
        lax.all_gather(attn_weight, "shard", axis=0, tiled=True),
        lax.all_gather(gains, "shard", axis=1, tiled=True),
        lax.all_gather(qk_gains, "shard", axis=1, tiled=True),
    )
    index = jnp.arange(token_rows, dtype=jnp.int32)
    valid = (index < counts[0]).astype(jnp.float32)[:, None]
    allowed = (index[None, :] <= index[:, None]) & (index[None, :] >= (index - positions)[:, None])
    gain_one = full_gains[0].astype(jnp.float32)
    gain_two = full_gains[1].astype(jnp.float32)
    query_gain = full_qk[0].astype(jnp.float32)
    k_gain = full_qk[1].astype(jnp.float32)
    wide = tokens.astype(jnp.float32)
    inv_one = lax.rsqrt(jnp.mean(wide * wide, axis=-1, keepdims=True) + EPS)
    unit_one = wide * inv_one
    normed_one = (unit_one * gain_one).astype(jnp.bfloat16)
    projected_output = jnp.dot(normed_one, full_attn[:, :width], preferred_element_type=jnp.float32)
    query = projected_output[:, :QUERY_FEATURES].reshape(token_rows, QUERY_HEADS, HEAD_WIDTH)
    key_rows = projected_output[:, QUERY_FEATURES : QUERY_FEATURES + KEY_FEATURES].reshape(
        token_rows, KEY_VALUE_HEADS, HEAD_WIDTH
    )
    value_rows = (
        projected_output[:, QUERY_FEATURES + KEY_FEATURES :]
        .reshape(token_rows, KEY_VALUE_HEADS, HEAD_WIDTH)
        .astype(jnp.bfloat16)
    )
    q_inv = lax.rsqrt(jnp.mean(query * query, axis=-1, keepdims=True) + EPS)
    query_unit = query * q_inv
    k_inv = lax.rsqrt(jnp.mean(key_rows * key_rows, axis=-1, keepdims=True) + EPS)
    k_unit = key_rows * k_inv
    cosine_table, sine_table = rope_tables(positions, HEAD_WIDTH)
    query_rotated = (
        apply_rotation(query_unit * query_gain, cosine_table, sine_table, 1.0)
        .astype(jnp.bfloat16)
        .reshape(token_rows, KEY_VALUE_HEADS, replica_group, HEAD_WIDTH)
    )
    key_r = apply_rotation(k_unit * k_gain, cosine_table, sine_table, 1.0).astype(jnp.bfloat16)
    scores = (
        jnp.einsum("qhgd,khd->hgqk", query_rotated, key_r, preferred_element_type=jnp.float32)
        * scale
    )
    masked = jnp.where(allowed, scores, -1e30)
    top = jnp.max(masked, axis=-1, keepdims=True)
    lse = top + jnp.log(jnp.sum(jnp.exp(masked - top), axis=-1, keepdims=True))
    probs = jnp.exp(masked - lse).astype(jnp.bfloat16)
    attended = jnp.einsum(
        "hgqk,khd->qhgd", probs, value_rows, preferred_element_type=jnp.float32
    ).astype(jnp.bfloat16)
    attended_flat = attended.reshape(token_rows, QUERY_FEATURES)
    mid = wide + times_trans(attended_flat, full_attn[:, width:])
    inv_two = lax.rsqrt(jnp.mean(mid * mid, axis=-1, keepdims=True) + EPS)
    unit_two = mid * inv_two
    normed_two = (unit_two * gain_two).astype(jnp.bfloat16)
    piece = lax.all_gather(ffn_weight, "shard", axis=0, tiled=True)
    gate = times_trans(normed_two, piece[:, 0, :])
    up_proj = times_trans(normed_two, piece[:, 1, :])
    hidden_piece = (gate * jax.nn.sigmoid(gate) * up_proj).astype(jnp.bfloat16)
    total = jnp.dot(hidden_piece, piece[:, 2, :], preferred_element_type=jnp.float32)
    gate_all = gate
    up_all = up_proj
    result = ((mid + total) * valid).astype(jnp.bfloat16)
    cot = (cotangent.astype(jnp.float32) * valid).astype(jnp.bfloat16)
    piece = lax.all_gather(ffn_weight, "shard", axis=0, tiled=True)
    gate = gate_all
    up_proj = up_all
    sig = jax.nn.sigmoid(gate)
    d_hidden = times_trans(cot, piece[:, 2, :])
    d_gate = (d_hidden * up_proj * sig * (1.0 + gate * (1.0 - sig))).astype(jnp.bfloat16)
    d_up = (d_hidden * gate * sig).astype(jnp.bfloat16)
    d_normed = jnp.dot(d_gate, piece[:, 0, :], preferred_element_type=jnp.float32) + jnp.dot(
        d_up, piece[:, 1, :], preferred_element_type=jnp.float32
    )
    grad_ffn = lax.psum_scatter(
        jnp.stack(
            [
                trans_times(d_gate, normed_two),
                trans_times(d_up, normed_two),
                trans_times(hidden_piece, cot),
            ],
            axis=1,
        ).astype(jnp.bfloat16),
        "shard",
        scatter_dimension=0,
        tiled=True,
    ).astype(jnp.float32)
    grad_two = jnp.sum(d_normed * unit_two, axis=0)
    d_mid = cot.astype(jnp.float32) + rms_back(d_normed, unit_two, inv_two, gain_two)
    d_mid_b = d_mid.astype(jnp.bfloat16)
    back_attn = lax.all_gather(attn_weight, "shard", axis=0, tiled=True)
    attended_gradient = jnp.dot(
        d_mid_b, back_attn[:, width:], preferred_element_type=jnp.float32
    ).astype(jnp.bfloat16)
    attention_gradient = attended_gradient.reshape(
        token_rows, KEY_VALUE_HEADS, replica_group, HEAD_WIDTH
    )
    scores_again = (
        jnp.einsum("qhgd,khd->hgqk", query_rotated, key_r, preferred_element_type=jnp.float32)
        * scale
    )
    probs_wide = jnp.exp(jnp.where(allowed, scores_again, -1e30) - lse)
    d_probs = jnp.einsum(
        "qhgd,khd->hgqk", attention_gradient, value_rows, preferred_element_type=jnp.float32
    )
    delta = jnp.sum(attention_gradient.astype(jnp.float32) * attended.astype(jnp.float32), axis=-1)
    delta = jnp.transpose(delta, (1, 2, 0))[..., None]
    d_scores = (probs_wide * (d_probs - delta) * scale).astype(jnp.bfloat16)
    d_query_r = jnp.einsum(
        "hgqk,khd->qhgd", d_scores, key_r, preferred_element_type=jnp.float32
    ).reshape(token_rows, QUERY_HEADS, HEAD_WIDTH)
    d_key_r = jnp.einsum(
        "hgqk,qhgd->khd", d_scores, query_rotated, preferred_element_type=jnp.float32
    )
    d_value = jnp.einsum(
        "hgqk,qhgd->khd", probs, attention_gradient, preferred_element_type=jnp.float32
    )
    d_q_scaled = apply_rotation(d_query_r, cosine_table, sine_table, -1.0)
    d_k_scaled = apply_rotation(d_key_r, cosine_table, sine_table, -1.0)
    grad_q = jnp.sum(d_q_scaled * query_unit, axis=(0, 1))
    grad_k = jnp.sum(d_k_scaled * k_unit, axis=(0, 1))
    d_query = rms_back(d_q_scaled, query_unit, q_inv, query_gain)
    d_key = rms_back(d_k_scaled, k_unit, k_inv, k_gain)
    d_projected = jnp.concatenate(
        [
            d_query.reshape(token_rows, QUERY_FEATURES),
            d_key.reshape(token_rows, KEY_FEATURES),
            d_value.reshape(token_rows, KEY_FEATURES),
        ],
        axis=1,
    ).astype(jnp.bfloat16)
    d_normed_one = times_trans(d_projected, back_attn[:, :width])
    grad_one = jnp.sum(d_normed_one * unit_one, axis=0)
    grad_input = (d_mid + rms_back(d_normed_one, unit_one, inv_one, gain_one)).astype(jnp.bfloat16)
    grad_attn = lax.psum_scatter(
        jnp.concatenate(
            [trans_times(normed_one, d_projected), trans_times(d_mid_b, attended_flat)], axis=1
        ).astype(jnp.bfloat16),
        "shard",
        scatter_dimension=0,
        tiled=True,
    ).astype(jnp.float32)
    grad_gains, grad_qk = (
        lax.psum_scatter(jnp.stack([grad_one, grad_two]), "shard", scatter_dimension=1, tiled=True),
        lax.psum_scatter(jnp.stack([grad_q, grad_k]), "shard", scatter_dimension=1, tiled=True),
    )
    grad_attn, grad_ffn, grad_gains, grad_qk = (
        lax.psum(grad_attn.astype(jnp.bfloat16), "rep").astype(jnp.float32),
        lax.psum(grad_ffn.astype(jnp.bfloat16), "rep").astype(jnp.float32),
        lax.psum(grad_gains.astype(jnp.bfloat16), "rep").astype(jnp.float32),
        lax.psum(grad_qk.astype(jnp.bfloat16), "rep").astype(jnp.float32),
    )
    return (result, grad_input, grad_attn, grad_ffn, grad_gains, grad_qk)


def solution(mesh):
    in_specs = (
        P(("rep", "shard"), None),
        P(("rep", "shard"), None),
        P(("rep", "shard")),
        P(("rep", "shard")),
        P("shard", None),
        P("shard", None, None),
        P(None, "shard"),
        P(None, "shard"),
    )
    out_specs = (
        P(("rep", "shard"), None),
        P(("rep", "shard"), None),
        P("shard", None),
        P("shard", None, None),
        P(None, "shard"),
        P(None, "shard"),
    )
    return jax.shard_map(local, mesh=mesh, in_specs=in_specs, out_specs=out_specs, check_vma=False)
```

profile of v0, /device:TPU:0, one launch (start us, length us, event | category | flops | bytes accessed | tf_op | source)
XLA Modules:
  0.0 899.5 jit_solution(8453053964591804986)
XLA Ops:
  8.7 13.5 %all-gather = bf16[8,8,2]{1,2,0:T(2,128)(2,1)S(1)} all-gather(bf16[1,8,2]{1,2,0:T(2,128)(2,1)S(1)} %bitcast.186), channel_id=1, replica_groups=mesh['rep'=4,'shard'=8] {'shard'}, dimensions={0}, use_global_device_ids=true | all-gather | bytes 288 | tf_op jit(solution)/shard_map/all_gather | solution.py:58
  23.1 9.1 %all_gather.14 = bf16[2,1024]{1,0:T(2,128)(2,1)S(1)} all-gather(bf16[2,128]{1,0:T(2,128)(2,1)S(1)} %copy-done.45), channel_id=1, replica_groups=mesh['rep'=4,'shard'=8] {'shard'}, dimensions={1}, use_global_device_ids=true | all-gather | bytes 4608 | tf_op jit(solution)/shard_map/all_gather | solution.py:57
  33.9 43.2 %all-gather.4.cloned.1.call-done = bf16[1024,3072]{1,0:T(8,128)(2,1)} async-done(((bf16[128,3072]{1,0:T(8,128)(2,1)}), bf16[1024,3072]{1,0:T(8,128)(2,1)}) %all-gather.4.cloned.1.call-update) | async-done | bytes 6291472 | tf_op jit(solution)/shard_map/all_gather | solution.py:56
  77.1 3.5 fusion.15
  90.6 3.1 multiply_reduce_fusion.5
  94.8 228.2 %all-gather.6.cloned.1.call-done = bf16[4608,3,1024]{2,0,1:T(8,128)(2,1)} async-done(((bf16[576,3,1024]{2,0,1:T(8,128)(2,1)}), bf16[4608,3,1024]{2,0,1:T(8,128)(2,1)}) %all-gather.6.cloned.1.call-update) | async-done | bytes 28311568 | tf_op jit(solution)/shard_map/all_gather | solution.py:108
  323.0 5.2 fusion.1
  328.3 8.6 fusion.3
  336.8 9.0 multiply_convert_fusion
  345.8 6.9 fusion
  352.8 6.2 multiply_reduce_fusion.1
  359.4 3.1 fusion.32
  365.9 4.3 fusion.35
  383.7 2.7 copy.84
  387.5 2.6 copy.86
  391.7 2.4 multiply_reduce_fusion
  396.3 3.3 pad_maximum_fusion.1
  400.6 6.9 fusion.7
  407.4 5.1 fusion.6
  412.6 5.2 fusion.8
  417.8 19.8 %pad_maximum_fusion = bf16[4608,3,1024]{2,0,1:T(8,128)(2,1)} fusion(bf16[4608,1,1024]{2,0,1:T(8,128)(2,1)} %fusion.8, bf16[4608,1,1024]{2,0,1:T(8,128)(2,1)} %fusion.7, bf16[4608,1,1024]{2,0,1:T(8,128)(2,1)} %fusion.6), kind=kLoop, calls=%fused_computation | loop fusion | flops 28311552 | bytes 56623104 | tf_op jit(solution)/shard_map/stack | solution.py:128
  438.8 4.6 fusion.42
  444.6 23.0 %reduce-scatter.7.cloned.1.call-done = bf16[128,3072]{1,0:T(8,128)(2,1)} async-done(((bf16[1024,3072]{1,0:T(8,128)(2,1)}), bf16[128,3072]{1,0:T(8,128)(2,1)}) %reduce-scatter.7.cloned.1.call-update) | async-done | bytes 786448 | tf_op jit(solution)/shard_map/reduce_scatter | solution.py:187
  467.6 277.4 %reduce-scatter.9.cloned.1.call-done = bf16[576,3,1024]{2,0,1:T(8,128)(2,1)} async-done(((bf16[4608,3,1024]{2,0,1:T(8,128)(2,1)}), bf16[576,3,1024]{2,0,1:T(8,128)(2,1)}) %reduce-scatter.9.cloned.1.call-update) | async-done | bytes 3538960 | tf_op jit(solution)/shard_map/reduce_scatter | solution.py:127
  746.5 13.7 %all-reduce = bf16[2,64]{1,0:T(2,128)(2,1)S(1)} all-reduce(f32[2,64]{1,0:T(2,128)S(1)} %pad_maximum_fusion.11), channel_id=5, replica_groups=mesh['rep'=4,'shard'=8] {'shard'}, use_global_device_ids=true, to_apply=%region_23.24.clone | all-reduce | flops 128 | bytes 768
  760.3 2.3 fusion.41
  762.6 7.9 fusion.31
  770.5 6.6 reduce-scatter.11.cloned.1.call-done
  778.0 9.9 %all-reduce.1 = (bf16[2,128]{1,0:T(2,128)(2,1)S(1)}, bf16[2,8]{1,0:T(2,128)(2,1)S(1)}) all-reduce(bf16[2,128]{1,0:T(2,128)(2,1)S(1)} %copy.108, bf16[2,8]{1,0:T(2,128)(2,1)S(1)} %dynamic-slice_convert_fusion), channel_id=1, replica_groups=mesh['rep'=4,'shard'=8] {'rep'}, use_global_device_ids=true, to_apply=%region_18.19 | all-reduce | flops 272 | bytes 1088 | tf_op jit(solution)/shard_map/psum | solution.py:202
  789.0 95.4 %all-reduce.5.cloned.1.call-done = (bf16[128,3072]{1,0:T(8,128)(2,1)}, bf16[576,3,1024]{2,0,1:T(8,128)(2,1)}) async-done(((bf16[128,3072]{1,0:T(8,128)(2,1)}, bf16[576,3,1024]{2,0,1:T(8,128)(2,1)}), (bf16[128,3072]{1,0:T(8,128)(2,1)}, bf16[576,3,1024]{2,0,1:T(8,128)(2,1)})) %all-reduce.5.cloned.1.call-update) | async-done | bytes 4325392 | tf_op jit(solution)/shard_map/psum | solution.py:200
  884.4 2.4 convert_element_type.149
  886.8 5.8 convert_element_type.150
  (179 shorter events, 42.7 us)
Async XLA Ops:
  7.2 16.0 %copy-start.45 = (bf16[2,128]{1,0:T(2,128)(2,1)S(1)}, bf16[2,128]{1,0:T(2,128)(2,1)}, u32[]{:S(2)}) copy-start(bf16[2,128]{1,0:T(2,128)(2,1)} %param.14) | copy-start | bytes 1540
  7.2 25.6 %copy-start.15 = (bf16[256,1024]{1,0:T(8,128)(2,1)S(1)}, bf16[256,1024]{1,0:T(8,128)(2,1)}, u32[]{:S(2)}) copy-start(bf16[256,1024]{1,0:T(8,128)(2,1)} %param.8) | copy-start | bytes 1572868
  7.2 25.8 %copy-start.43 = (s32[256]{0:T(256)S(1)}, s32[256]{0:T(256)}, u32[]{:S(2)}) copy-start(s32[256]{0:T(256)} %param.10) | copy-start | bytes 3076
  7.2 69.9 %all-gather.4.cloned.1.call-start = ((), (), s32[]{:S(2)}) async-start(), calls=%async_computation.3 | async-start | bytes 7077888 | tf_op jit(solution)/shard_map/all_gather | solution.py:56
  7.9 315.1 %all-gather.6.cloned.1.call-start = ((), (), s32[]{:S(2)}) async-start(), calls=%async_computation.4 | async-start | bytes 31850496 | tf_op jit(solution)/shard_map/all_gather | solution.py:108
  8.7 458.9 %reduce-scatter.7.cloned.1.call-start = ((), (), s32[]{:S(2)}) async-start(), calls=%async_computation.5 | async-start | bytes 7077888 | tf_op jit(solution)/shard_map/reduce_scatter | solution.py:187
  33.0 47.6 %copy-start.38 = (f32[256]{0:T(256)}, f32[256]{0:T(256)S(1)}, u32[]{:S(2)}) copy-start(f32[256]{0:T(256)S(1)} %add_rsqrt_fusion.3) | copy-start | bytes 3076
  94.8 233.4 %copy-start.3 = (bf16[256,1024]{1,0:T(8,128)(2,1)}, bf16[256,1024]{1,0:T(8,128)(2,1)S(1)}, u32[]{:S(2)}) copy-start(bf16[256,1024]{1,0:T(8,128)(2,1)S(1)} %multiply_convert_fusion.5) | copy-start | bytes 1572868
  328.2 8.6 copy-start.19
  328.3 8.6 copy-start.41
  345.8 6.9 copy-start.10
  345.8 6.9 copy-start.12
  345.8 6.9 copy-start.6
  359.0 7.0 copy-start.37
  364.5 5.7 copy-start.9
  364.5 5.7 copy-start.14
  364.5 5.7 copy-start.30
  364.6 5.7 copy-start.34
  383.7 6.3 copy-start.2
  387.5 7.4 copy-start.39
  390.1 4.8 copy-start.17
  390.1 4.8 copy-start.31
  399.5 345.5 %reduce-scatter.9.cloned.1.call-start = ((), (), s32[]{:S(2)}) async-start(), calls=%async_computation.6 | async-start | bytes 31850496 | tf_op jit(solution)/shard_map/reduce_scatter | solution.py:127
  400.6 6.9 copy-start.11
  407.4 5.2 copy-start.13
  407.4 5.2 copy-start.20
  407.4 5.2 copy-start.42
  437.6 5.8 copy-start.40
  437.6 339.5 %reduce-scatter.11.cloned.1.call-start = ((), (), s32[]{:S(2)}) async-start(), calls=%async_computation.7 | async-start | bytes 589824
  443.4 301.6 %copy-start.46 = (u32[32]{0:T(128)S(1)}, u32[32]{0:T(128)}, u32[]{:S(2)}) copy-start(u32[32]{0:T(128)} %constant.39) | copy-start | bytes 388
  443.4 319.2 %copy-start.7 = (f32[256,1024]{1,0:T(8,128)S(1)}, f32[256,1024]{1,0:T(8,128)}, u32[]{:S(2)}) copy-start(f32[256,1024]{1,0:T(8,128)} %copy-done.5) | copy-start | bytes 3145732
  444.5 439.9 %all-reduce.5.cloned.1.call-start = ((), (), s32[]{:S(2)}) async-start(), calls=%async_computation.8 | async-start | bytes 8650752 | tf_op jit(solution)/shard_map/psum | solution.py:200
  (21 other events, 40.0 us)
Sparse Core Ops, SparseCore 0:
  9.7 67.3 all-gather.3
  78.7 244.2 all-gather.5
  399.7 67.8 reduce-scatter.6
  469.8 275.1 reduce-scatter.8
  747.1 29.9 reduce-scatter.10
  780.5 103.8 all-reduce.4
where the time goes:
time: 900 us; the launch traced here: 899 us
  waiting for transfers between devices  675 us (75%)
  matrix products  90.3 us (10%)
  other arithmetic  47.9 us (5%)
  blocking collectives  46.2 us (5%)
  local copies, waits for them, and re-layouts  23.5 us (3%)
  between operations  16.1 us (2%)
    reduce_scatter x1, waiting for transfers between devices, local(): lax.psum_scatter(jnp.stack([trans_times(d_gate, normed_two), trans_times(...  277 us
    all_gather x1, waiting for transfers between devices, local(): piece = lax.all_gather(ffn_weight, 'shard', axis=0, tiled=True)  228 us
    psum x1, waiting for transfers between devices, local(): lax.psum(grad_attn.astype(jnp.bfloat16), 'rep').astype(jnp.float32)  95.4 us
    all_gather x1, waiting for transfers between devices, local(): lax.all_gather(attn_weight, 'shard', axis=0, tiled=True)  43.2 us
    dot_general x5, matrix products, times_trans(): lax.dot_general(left, right, (((1,), (1,)), ((), ())), preferred_element_...  30.4 us
    reduce_scatter x1, waiting for transfers between devices, local(): lax.psum_scatter(jnp.concatenate([trans_times(normed_one, d_projected), t...  23 us
    dot_general x5, matrix products, trans_times(): lax.dot_general(left, right, (((0,), (0,)), ((), ())), preferred_element_...  20.6 us
    another operation x1, other arithmetic, local(): jnp.stack([trans_times(d_gate, normed_two), trans_times(d_up, normed_two)...  19.8 us
  transfers between devices with their start and end apart: 6, of which 6 were waited for; matrix products, arithmetic and copies ran while one was open for 8% of the time, Pallas kernels for 0%

commit v1 on v0

--- a/solution.py
+++ b/solution.py
@@ -12,6 +12,8 @@
 
 EPS = 1e-05
 THETA = 1000000.0
+CHUNKS = 2
+BOTH = ("rep", "shard")
 
 
 def rope_tables(positions, head_size):
@@ -52,11 +54,32 @@
     width = QUERY_FEATURES + 2 * KEY_FEATURES
     replica_group = QUERY_HEADS // KEY_VALUE_HEADS
     scale = HEAD_WIDTH ** (-0.5)
-    full_attn, full_gains, full_qk = (
-        lax.all_gather(attn_weight, "shard", axis=0, tiled=True),
-        lax.all_gather(gains, "shard", axis=1, tiled=True),
-        lax.all_gather(qk_gains, "shard", axis=1, tiled=True),
-    )
+    reps, shards = lax.axis_size("rep"), lax.axis_size("shard")
+    group, member = lax.axis_index("rep"), lax.axis_index("shard")
+    attn_rows = attn_weight.shape[0] // reps
+    attn_cols = attn_weight.shape[1]
+    full_attn = lax.all_gather(
+        lax.dynamic_slice_in_dim(attn_weight, group * attn_rows, attn_rows, 0), BOTH, axis=0
+    )
+    full_attn = (
+        full_attn.reshape(reps, shards, attn_rows, attn_cols)
+        .transpose(1, 0, 2, 3)
+        .reshape(-1, attn_cols)
+    )
+    gain_cols, qk_cols = gains.shape[1], qk_gains.shape[1]
+    scales = lax.all_gather(jnp.concatenate([gains, qk_gains], axis=1), "shard", axis=1)
+    full_gains = scales[:, :, :gain_cols].reshape(2, -1)
+    full_qk = scales[:, :, gain_cols:].reshape(2, -1)
+    ffn_rows = ffn_weight.shape[0] // reps // CHUNKS
+    pieces = [
+        lax.all_gather(
+            lax.dynamic_slice_in_dim(ffn_weight, (group * CHUNKS + c) * ffn_rows, ffn_rows, 0),
+            BOTH,
+            axis=0,
+            tiled=True,
+        )
+        for c in range(CHUNKS)
+    ]
     index = jnp.arange(token_rows, dtype=jnp.int32)
     valid = (index < counts[0]).astype(jnp.float32)[:, None]
     allowed = (index[None, :] <= index[:, None]) & (index[None, :] >= (index - positions)[:, None])
@@ -105,44 +128,49 @@
     inv_two = lax.rsqrt(jnp.mean(mid * mid, axis=-1, keepdims=True) + EPS)
     unit_two = mid * inv_two
     normed_two = (unit_two * gain_two).astype(jnp.bfloat16)
-    piece = lax.all_gather(ffn_weight, "shard", axis=0, tiled=True)
-    gate = times_trans(normed_two, piece[:, 0, :])
-    up_proj = times_trans(normed_two, piece[:, 1, :])
-    hidden_piece = (gate * jax.nn.sigmoid(gate) * up_proj).astype(jnp.bfloat16)
-    total = jnp.dot(hidden_piece, piece[:, 2, :], preferred_element_type=jnp.float32)
-    gate_all = gate
-    up_all = up_proj
+    cot = (cotangent.astype(jnp.float32) * valid).astype(jnp.bfloat16)
+    total = 0.0
+    d_normed = 0.0
+    ffn_terms = []
+    for piece in pieces:
+        gate = times_trans(normed_two, piece[:, 0, :])
+        up_proj = times_trans(normed_two, piece[:, 1, :])
+        d_hidden = times_trans(cot, piece[:, 2, :])
+        sig = jax.nn.sigmoid(gate)
+        act = gate * sig
+        hidden_piece = (act * up_proj).astype(jnp.bfloat16)
+        d_gate = (d_hidden * up_proj * sig * (1.0 + gate * (1.0 - sig))).astype(jnp.bfloat16)
+        d_up = (d_hidden * act).astype(jnp.bfloat16)
+        ffn_terms.append(
+            lax.psum_scatter(
+                jnp.stack(
+                    [
+                        trans_times(d_gate, normed_two).astype(jnp.bfloat16),
+                        trans_times(d_up, normed_two).astype(jnp.bfloat16),
+                        trans_times(hidden_piece, cot).astype(jnp.bfloat16),
+                    ],
+                    axis=1,
+                ),
+                BOTH,
+                scatter_dimension=0,
+                tiled=True,
+            )
+        )
+        total = total + jnp.dot(hidden_piece, piece[:, 2, :], preferred_element_type=jnp.float32)
+        d_normed = (
+            d_normed
+            + jnp.dot(d_gate, piece[:, 0, :], preferred_element_type=jnp.float32)
+            + jnp.dot(d_up, piece[:, 1, :], preferred_element_type=jnp.float32)
+        )
     result = ((mid + total) * valid).astype(jnp.bfloat16)
-    cot = (cotangent.astype(jnp.float32) * valid).astype(jnp.bfloat16)
-    piece = lax.all_gather(ffn_weight, "shard", axis=0, tiled=True)
-    gate = gate_all
-    up_proj = up_all
-    sig = jax.nn.sigmoid(gate)
-    d_hidden = times_trans(cot, piece[:, 2, :])
-    d_gate = (d_hidden * up_proj * sig * (1.0 + gate * (1.0 - sig))).astype(jnp.bfloat16)
-    d_up = (d_hidden * gate * sig).astype(jnp.bfloat16)
-    d_normed = jnp.dot(d_gate, piece[:, 0, :], preferred_element_type=jnp.float32) + jnp.dot(
-        d_up, piece[:, 1, :], preferred_element_type=jnp.float32
-    )
-    grad_ffn = lax.psum_scatter(
-        jnp.stack(
-            [
-                trans_times(d_gate, normed_two),
-                trans_times(d_up, normed_two),
-                trans_times(hidden_piece, cot),
-            ],
-            axis=1,
-        ).astype(jnp.bfloat16),
-        "shard",
-        scatter_dimension=0,
-        tiled=True,
+    grad_ffn = lax.all_gather(
+        jnp.concatenate(ffn_terms, axis=0), "rep", axis=0, tiled=True
     ).astype(jnp.float32)
     grad_two = jnp.sum(d_normed * unit_two, axis=0)
     d_mid = cot.astype(jnp.float32) + rms_back(d_normed, unit_two, inv_two, gain_two)
     d_mid_b = d_mid.astype(jnp.bfloat16)
-    back_attn = lax.all_gather(attn_weight, "shard", axis=0, tiled=True)
     attended_gradient = jnp.dot(
-        d_mid_b, back_attn[:, width:], preferred_element_type=jnp.float32
+        d_mid_b, full_attn[:, width:], preferred_element_type=jnp.float32
     ).astype(jnp.bfloat16)
     attention_gradient = attended_gradient.reshape(
         token_rows, KEY_VALUE_HEADS, replica_group, HEAD_WIDTH
@@ -181,27 +209,33 @@
         ],
         axis=1,
     ).astype(jnp.bfloat16)
-    d_normed_one = times_trans(d_projected, back_attn[:, :width])
+    d_normed_one = times_trans(d_projected, full_attn[:, :width])
     grad_one = jnp.sum(d_normed_one * unit_one, axis=0)
     grad_input = (d_mid + rms_back(d_normed_one, unit_one, inv_one, gain_one)).astype(jnp.bfloat16)
-    grad_attn = lax.psum_scatter(
-        jnp.concatenate(
-            [trans_times(normed_one, d_projected), trans_times(d_mid_b, attended_flat)], axis=1
-        ).astype(jnp.bfloat16),
-        "shard",
-        scatter_dimension=0,
+    attn_terms = jnp.concatenate(
+        [
+            trans_times(normed_one, d_projected).astype(jnp.bfloat16),
+            trans_times(d_mid_b, attended_flat).astype(jnp.bfloat16),
+        ],
+        axis=1,
+    )
+    attn_terms = (
+        attn_terms.reshape(shards, reps, attn_rows, attn_cols)
+        .transpose(1, 0, 2, 3)
+        .reshape(-1, attn_cols)
+    )
+    grad_attn = lax.all_gather(
+        lax.psum_scatter(attn_terms, BOTH, scatter_dimension=0, tiled=True),
+        "rep",
+        axis=0,
         tiled=True,
     ).astype(jnp.float32)
-    grad_gains, grad_qk = (
-        lax.psum_scatter(jnp.stack([grad_one, grad_two]), "shard", scatter_dimension=1, tiled=True),
-        lax.psum_scatter(jnp.stack([grad_q, grad_k]), "shard", scatter_dimension=1, tiled=True),
-    )
-    grad_attn, grad_ffn, grad_gains, grad_qk = (
-        lax.psum(grad_attn.astype(jnp.bfloat16), "rep").astype(jnp.float32),
-        lax.psum(grad_ffn.astype(jnp.bfloat16), "rep").astype(jnp.float32),
-        lax.psum(grad_gains.astype(jnp.bfloat16), "rep").astype(jnp.float32),
-        lax.psum(grad_qk.astype(jnp.bfloat16), "rep").astype(jnp.float32),
-    )
+    small = lax.psum(
+        jnp.concatenate([jnp.stack([grad_one, grad_two]), jnp.stack([grad_q, grad_k])], axis=1),
+        BOTH,
+    )
+    grad_gains = lax.dynamic_slice_in_dim(small, member * gain_cols, gain_cols, 1)
+    grad_qk = lax.dynamic_slice_in_dim(small, QUERY_FEATURES + member * qk_cols, qk_cols, 1)
     return (result, grad_input, grad_attn, grad_ffn, grad_gains, grad_qk)
 
 

time: 900 us -> 818 us (0.909); the launches traced: 899 us -> 808 us
  waiting for transfers between devices: 675 us -> 558 us
  local copies, waits for them, and re-layouts: 23.5 us -> 46.2 us
  blocking collectives: 46.2 us -> 66.8 us
  other arithmetic: 47.9 us -> 30.9 us
    reduce_scatter x2 -> x1, waiting for transfers between devices: 300 us -> 62.3 us  [local(): lax.psum_scatter(attn_terms, BOTH, scatter_dimension=0, tiled=True)]
    unnamed x7 -> x9, waiting for transfers between devices: 8.03 us -> 241 us
    psum x1 -> x0, waiting for transfers between devices: 95.4 us -> none  [local(): lax.psum(grad_attn.astype(jnp.bfloat16), 'rep').astype(jnp.float32)]
    psum x1, blocking collectives: 9.88 us -> 39.7 us  [local(): lax.psum(jnp.concatenate([jnp.stack([grad_one, grad_two]), jnp.stack([gra...]
    another operation x5 -> x2, other arithmetic: 20 us -> 0.22 us  [the longest x1 19.8 us: local(): jnp.stack([trans_times(d_gate, normed_two), trans_times(d_up, normed_two)...]
    all_gather x2 -> x4, waiting for transfers between devices: 271 us -> 255 us  [the longest x2 169 us: local(): lax.all_gather(lax.dynamic_slice_in_dim(ffn_weight, (group * CHUNKS + c)...]
    unnamed x1 -> x0, blocking collectives: 13.7 us -> none
    unnamed x98 -> x91, local copies, waits for them, and re-layouts: 7.91 us -> 20.1 us
  transfers between devices with their start and end apart: 6 -> 7, of which waited for: 6 -> 7; matrix products, arithmetic and copies ran while one was open for 8% -> 19% of each run, Pallas kernels for 0% -> 0%
where the time goes in v1:
time: 818 us; the launch traced here: 808 us
  waiting for transfers between devices  558 us (68%)
  matrix products  90.3 us (11%)
  blocking collectives  66.8 us (8%)
  local copies, waits for them, and re-layouts  46.2 us (6%)
  other arithmetic  30.9 us (4%)
  between operations  15.9 us (2%)
    unnamed x9, waiting for transfers between devices  241 us
    all_gather x2, waiting for transfers between devices, local(): lax.all_gather(lax.dynamic_slice_in_dim(ffn_weight, (group * CHUNKS + c)...  169 us
    reduce_scatter x1, waiting for transfers between devices, local(): lax.psum_scatter(attn_terms, BOTH, scatter_dimension=0, tiled=True)  62.3 us
    all_gather x1, waiting for transfers between devices, local(): lax.all_gather(lax.dynamic_slice_in_dim(attn_weight, group * attn_rows, a...  53 us
    psum x1, blocking collectives, local(): lax.psum(jnp.concatenate([jnp.stack([grad_one, grad_two]), jnp.stack([gra...  39.7 us
    all_gather x1, waiting for transfers between devices, local(): lax.all_gather(jnp.concatenate(ffn_terms, axis=0), 'rep', axis=0, tiled=T...  33.1 us
    dot_general x8, matrix products, times_trans(): lax.dot_general(left, right, (((1,), (1,)), ((), ())), preferred_element_...  30.8 us
    unnamed x91, local copies, waits for them, and re-layouts  20.1 us
  transfers between devices with their start and end apart: 7, of which 7 were waited for; matrix products, arithmetic and copies ran while one was open for 19% of the time, Pallas kernels for 0%

profile of v1, /device:TPU:0, one launch (start us, length us, event | category | flops | bytes accessed | tf_op | source)
XLA Modules:
  0.0 808.4 jit_solution(9696144375495831040)
XLA Ops:
  12.7 13.5 %all-gather.2 = bf16[8,136,2]{1,2,0:T(2,128)(2,1)S(1)} all-gather(bf16[1,136,2]{1,2,0:T(2,128)(2,1)S(1)} %maximum_bitcast_fusion.5), channel_id=2, replica_groups=mesh['rep'=4,'shard'=8] {'shard'}, dimensions={0}, use_global_device_ids=true | all-gather | bytes 4896 | tf_op jit(solution)/shard_map/all_gather | solution.py:70
  30.7 53.0 %all-gather.14.cloned.1.call-done = bf16[1024,3072]{1,0:T(8,128)(2,1)} async-done(((bf16[32,3072]{1,0:T(8,128)(2,1)}), bf16[1024,3072]{1,0:T(8,128)(2,1)}) %all-gather.14.cloned.1.call-update) | async-done | bytes 6291472 | tf_op jit(solution)/shard_map/all_gather | solution.py:61
  83.7 3.3 copy.104
  99.3 89.2 %all-gather.10.cloned.1.call-done = bf16[2304,3,1024]{2,0,1:T(8,128)(2,1)} async-done(((bf16[72,3,1024]{2,0,1:T(8,128)(2,1)}), bf16[2304,3,1024]{2,0,1:T(8,128)(2,1)}) %all-gather.10.cloned.1.call-update) | async-done | bytes 14155792 | tf_op jit(solution)/shard_map/all_gather | solution.py:75
  188.5 3.8 fusion.16
  192.3 3.8 fusion.18
  196.2 4.6 multiply_convert_fusion
  207.5 6.1 copy.142
  213.7 79.6 %all-gather.8.cloned.1.call-done = bf16[2304,3,1024]{2,0,1:T(8,128)(2,1)} async-done(((bf16[72,3,1024]{2,0,1:T(8,128)(2,1)}), bf16[2304,3,1024]{2,0,1:T(8,128)(2,1)}) %all-gather.8.cloned.1.call-update) | async-done | bytes 14155792 | tf_op jit(solution)/shard_map/all_gather | solution.py:75
  293.3 3.8 fusion.10
  297.1 3.8 fusion.12
  300.9 4.7 multiply_convert_fusion.2
  311.9 6.0 copy.141
  321.2 4.5 fusion.9
  325.8 4.2 fusion.42
  330.0 4.3 fusion.41
  334.3 4.9 multiply_reduce_fusion.1
  344.9 4.1 fusion.49
  352.0 4.6 fusion.8
  376.8 3.4 convolution_convert_fusion.6
  380.2 3.4 pad_maximum_fusion
  383.6 3.3 copy.123
  387.0 73.3 %reduce-scatter.12.cloned.1.call-done = bf16[72,3072]{1,0:T(8,128)(2,1)} async-done(((bf16[2304,3072]{1,0:T(8,128)(2,1)}), bf16[72,3072]{1,0:T(8,128)(2,1)}) %reduce-scatter.12.cloned.1.call-update) | async-done | bytes 442384
  461.4 166.6 %reduce-scatter.10.cloned.1.call-done = bf16[72,3072]{1,0:T(8,128)(2,1)} async-done(((bf16[2304,3072]{1,0:T(8,128)(2,1)}), bf16[72,3072]{1,0:T(8,128)(2,1)}) %reduce-scatter.10.cloned.1.call-update) | async-done | bytes 442384
  630.2 3.8 fusion.56
  634.0 39.7 %psum.7 = f32[2,1088]{1,0:T(2,128)S(1)} all-reduce(f32[2,1088]{1,0:T(2,128)S(1)} %maximum_maximum_fusion), channel_id=1, replica_groups=mesh['rep'=4,'shard'=8] {'rep','shard'}, use_global_device_ids=true, to_apply=%region_20.21 | all-reduce | flops 2176 | bytes 17408 | tf_op jit(solution)/shard_map/psum | solution.py:233
  676.1 4.2 fusion.14
  680.4 4.8 fusion.48
  685.2 62.3 %reduce-scatter.8.cloned.1.call-done = bf16[32,3072]{1,0:T(8,128)(2,1)} async-done(((bf16[1024,3072]{1,0:T(8,128)(2,1)}), bf16[32,3072]{1,0:T(8,128)(2,1)}) %reduce-scatter.8.cloned.1.call-update) | async-done | bytes 196624 | tf_op jit(solution)/shard_map/reduce_scatter | solution.py:228
  747.5 13.6 %all_gather.30 = bf16[128,3072]{1,0:T(8,128)(2,1)S(1)} all-gather(bf16[32,3072]{1,0:T(8,128)(2,1)} %reduce-scatter.8.cloned.1.call-done), channel_id=1, replica_groups=mesh['rep'=4,'shard'=8] {'rep'}, dimensions={0}, use_global_device_ids=true | all-gather | bytes 983040 | tf_op jit(solution)/shard_map/all_gather | solution.py:227
  762.4 33.1 %all-gather.12.cloned.1.call-done = bf16[576,3,1024]{2,0,1:T(8,128)(2,1)} async-done(((bf16[144,3,1024]{2,0,1:T(8,128)(2,1)}), bf16[576,3,1024]{2,0,1:T(8,128)(2,1)}) %all-gather.12.cloned.1.call-update) | async-done | bytes 3538960 | tf_op jit(solution)/shard_map/all_gather | solution.py:166
  795.5 5.8 convert_element_type.196
  (191 shorter events, 73.6 us)
Async XLA Ops:
  7.2 76.5 %all-gather.14.cloned.1.call-start = ((), (), s32[]{:S(2)}) async-start(), calls=%async_computation.7 | async-start | bytes 6488064 | tf_op jit(solution)/shard_map/all_gather | solution.py:61
  9.0 179.5 %all-gather.10.cloned.1.call-start = ((), (), s32[]{:S(2)}) async-start(), calls=%async_computation.4 | async-start | bytes 14598144 | tf_op jit(solution)/shard_map/all_gather | solution.py:75
  11.2 282.1 %all-gather.8.cloned.1.call-start = ((), (), s32[]{:S(2)}) async-start(), calls=%async_computation.3 | async-start | bytes 14598144 | tf_op jit(solution)/shard_map/all_gather | solution.py:75
  12.0 448.4 %reduce-scatter.12.cloned.1.call-start = ((), (), s32[]{:S(2)}) async-start(), calls=%async_computation.9 | async-start | bytes 14598144
  26.5 65.7 %copy-start.37 = (f32[64]{0:T(128)}, f32[64]{0:T(128)S(1)}, u32[]{:S(2)}) copy-start(f32[64]{0:T(128)S(1)} %reshape.254) | copy-start | bytes 772
  26.5 65.4 %copy-start.35 = (f32[64]{0:T(128)}, f32[64]{0:T(128)S(1)}, u32[]{:S(2)}) copy-start(f32[64]{0:T(128)S(1)} %reshape.253) | copy-start | bytes 772
  29.0 57.9 %copy-start.40 = (f32[256]{0:T(256)}, f32[256]{0:T(256)S(1)}, u32[]{:S(2)}) copy-start(f32[256]{0:T(256)S(1)} %add_rsqrt_fusion.3) | copy-start | bytes 3076
  83.7 3.3 copy-start.23
  192.3 3.8 copy-start.5
  192.3 3.8 copy-start.34
  200.7 3.3 copy-start.11
  200.7 3.3 copy-start.13
  200.8 3.3 copy-start.18
  213.7 414.3 %reduce-scatter.10.cloned.1.call-start = ((), (), s32[]{:S(2)}) async-start(), calls=%async_computation.8 | async-start | bytes 14598144
  317.9 429.5 %reduce-scatter.8.cloned.1.call-start = ((), (), s32[]{:S(2)}) async-start(), calls=%async_computation.5 | async-start | bytes 6488064 | tf_op jit(solution)/shard_map/reduce_scatter | solution.py:228
  321.2 4.6 copy-start.16
  325.8 4.2 copy-start.14
  329.9 4.3 copy-start.7
  330.0 4.3 copy-start.12
  342.8 8.0 copy-start.22
  352.0 6.0 copy-start.28
  359.7 5.5 copy-start.39
  365.2 5.2 copy-start.26
  370.4 3.8 copy-start.10
  372.0 4.7 copy-start.25
  372.0 4.7 copy-start.32
  372.1 4.7 copy-start.41
  387.0 408.6 %all-gather.12.cloned.1.call-start = ((), (), s32[]{:S(2)}) async-start(), calls=%async_computation.6 | async-start | bytes 4423680 | tf_op jit(solution)/shard_map/all_gather | solution.py:166
  630.2 3.8 copy-start.42
  676.1 4.2 copy-start.8
  676.1 4.2 copy-start.19
  761.1 40.3 %copy-start.1 = (bf16[128,3072]{1,0:T(8,128)(2,1)S(1)}, bf16[128,3072]{1,0:T(8,128)(2,1)}, u32[]{:S(2)}) copy-start(bf16[128,3072]{1,0:T(8,128)(2,1)} %param.12) | copy-start | bytes 2359300
  (18 other events, 31.3 us)
Sparse Core Ops, SparseCore 0:
  11.6 72.0 all-gather.13
  87.4 101.0 all-gather.9
  192.3 100.9 all-gather.7
  299.2 161.1 reduce-scatter.11
  466.2 161.6 reduce-scatter.9
  633.4 114.0 reduce-scatter.7
  749.3 46.1 all-gather.11

commit v2 on v1

--- a/solution.py
+++ b/solution.py
@@ -12,7 +12,7 @@
 
 EPS = 1e-05
 THETA = 1000000.0
-CHUNKS = 2
+CHUNKS = 1
 BOTH = ("rep", "shard")
 
 
@@ -49,6 +49,17 @@
     )
 
 
+def swap_cores(array, devices):
+    return lax.ppermute(array, BOTH, [(i, i + 1 - 2 * (i % 2)) for i in range(devices)])
+
+
+def scatter_cores(array, devices):
+    groups = [list(range(0, devices, 2)), list(range(1, devices, 2))]
+    return lax.psum_scatter(
+        array, BOTH, scatter_dimension=0, axis_index_groups=groups, tiled=True
+    )
+
+
 def local(tokens, cotangent, positions, counts, attn_weight, ffn_weight, gains, qk_gains):
     token_rows = tokens.shape[0]
     width = QUERY_FEATURES + 2 * KEY_FEATURES
@@ -56,6 +67,7 @@
     scale = HEAD_WIDTH ** (-0.5)
     reps, shards = lax.axis_size("rep"), lax.axis_size("shard")
     group, member = lax.axis_index("rep"), lax.axis_index("shard")
+    core = lax.rem(member, 2)
     attn_rows = attn_weight.shape[0] // reps
     attn_cols = attn_weight.shape[1]
     full_attn = lax.all_gather(
@@ -141,21 +153,27 @@
         hidden_piece = (act * up_proj).astype(jnp.bfloat16)
         d_gate = (d_hidden * up_proj * sig * (1.0 + gate * (1.0 - sig))).astype(jnp.bfloat16)
         d_up = (d_hidden * act).astype(jnp.bfloat16)
-        ffn_terms.append(
-            lax.psum_scatter(
-                jnp.stack(
-                    [
-                        trans_times(d_gate, normed_two).astype(jnp.bfloat16),
-                        trans_times(d_up, normed_two).astype(jnp.bfloat16),
-                        trans_times(hidden_piece, cot).astype(jnp.bfloat16),
-                    ],
-                    axis=1,
-                ),
-                BOTH,
-                scatter_dimension=0,
-                tiled=True,
-            )
-        )
+        columns = [
+            h.reshape(token_rows, reps * shards // 2, 2, ffn_rows)
+            for h in (d_gate, d_up, hidden_piece)
+        ]
+
+        def terms_of(which):
+            halves = [
+                lax.dynamic_index_in_dim(h, which, 2, keepdims=False).reshape(token_rows, -1)
+                for h in columns
+            ]
+            return [
+                trans_times(h, other) for h, other in zip(halves, (normed_two, normed_two, cot))
+            ]
+
+        sent = [t.astype(jnp.bfloat16) for t in terms_of(1 - core)]
+        arrived = [swap_cores(t, reps * shards) for t in sent]
+        kept = [
+            (t + a.astype(jnp.float32)).astype(jnp.bfloat16)
+            for t, a in zip(terms_of(core), arrived)
+        ]
+        ffn_terms.append(scatter_cores(jnp.stack(kept, axis=1), reps * shards))
         total = total + jnp.dot(hidden_piece, piece[:, 2, :], preferred_element_type=jnp.float32)
         d_normed = (
             d_normed
@@ -163,9 +181,6 @@
             + jnp.dot(d_up, piece[:, 1, :], preferred_element_type=jnp.float32)
         )
     result = ((mid + total) * valid).astype(jnp.bfloat16)
-    grad_ffn = lax.all_gather(
-        jnp.concatenate(ffn_terms, axis=0), "rep", axis=0, tiled=True
-    ).astype(jnp.float32)
     grad_two = jnp.sum(d_normed * unit_two, axis=0)
     d_mid = cot.astype(jnp.float32) + rms_back(d_normed, unit_two, inv_two, gain_two)
     d_mid_b = d_mid.astype(jnp.bfloat16)
@@ -218,22 +233,26 @@
             trans_times(d_mid_b, attended_flat).astype(jnp.bfloat16),
         ],
         axis=1,
-    )
-    attn_terms = (
-        attn_terms.reshape(shards, reps, attn_rows, attn_cols)
-        .transpose(1, 0, 2, 3)
-        .reshape(-1, attn_cols)
-    )
-    grad_attn = lax.all_gather(
-        lax.psum_scatter(attn_terms, BOTH, scatter_dimension=0, tiled=True),
-        "rep",
-        axis=0,
-        tiled=True,
+    ).reshape(shards // 2, 2, reps, attn_rows, attn_cols)
+
+    def attn_half(which):
+        half = lax.dynamic_index_in_dim(attn_terms, which, 1, keepdims=False)
+        return half.transpose(1, 0, 2, 3).reshape(-1, attn_cols)
+
+    attn_kept = (
+        attn_half(core).astype(jnp.float32)
+        + swap_cores(attn_half(1 - core), reps * shards).astype(jnp.float32)
+    ).astype(jnp.bfloat16)
+    small = jnp.concatenate(
+        [jnp.stack([grad_one, grad_two]), jnp.stack([grad_q, grad_k])], axis=1
+    )
+    attn_kept, small, ffn_terms = lax.optimization_barrier((attn_kept, small, ffn_terms))
+    grad_attn = scatter_cores(attn_kept, reps * shards)
+    grad_ffn = lax.all_gather(
+        jnp.concatenate(ffn_terms, axis=0), "rep", axis=0, tiled=True
     ).astype(jnp.float32)
-    small = lax.psum(
-        jnp.concatenate([jnp.stack([grad_one, grad_two]), jnp.stack([grad_q, grad_k])], axis=1),
-        BOTH,
-    )
+    grad_attn = lax.all_gather(grad_attn, "rep", axis=0, tiled=True).astype(jnp.float32)
+    small = lax.psum(small, BOTH)
     grad_gains = lax.dynamic_slice_in_dim(small, member * gain_cols, gain_cols, 1)
     grad_qk = lax.dynamic_slice_in_dim(small, QUERY_FEATURES + member * qk_cols, qk_cols, 1)
     return (result, grad_input, grad_attn, grad_ffn, grad_gains, grad_qk)

time: 818 us -> 750 us (0.917)
  waiting for transfers between devices: 558 us -> 486 us
    unnamed x9 -> x5, waiting for transfers between devices: 241 us -> 0.6 us
    reduce_scatter x1 -> x2, waiting for transfers between devices: 62.3 us -> 273 us  [scatter_cores(): lax.psum_scatter(array, BOTH, scatter_dimension=0, axis_index_groups=grou...]
    all_gather x1, waiting for transfers between devices: 33.1 us -> 0.01 us  [local(): lax.all_gather(jnp.concatenate(ffn_terms, axis=0), 'rep', axis=0, tiled=T...]
    all_gather x2 -> x1, waiting for transfers between devices: 169 us -> 154 us  [local(): lax.all_gather(lax.dynamic_slice_in_dim(ffn_weight, (group * CHUNKS + c)...]
    convert_element_type x0 -> x4, local copies, waits for them, and re-layouts: none -> 13.2 us  [the longest x1 4.28 us: local(): d_up = (d_hidden * act).astype(jnp.bfloat16)]
    unnamed x91 -> x101, local copies, waits for them, and re-layouts: 20.1 us -> 7.57 us
    dot_general x8, matrix products: 14.5 us -> 23 us  [trans_times(): lax.dot_general(left, right, (((0,), (0,)), ((), ())), preferred_element_...]
    dot_general x8 -> x5, matrix products: 30.8 us -> 27.7 us  [times_trans(): lax.dot_general(left, right, (((1,), (1,)), ((), ())), preferred_element_...]
  transfers between devices with their start and end apart: 7 -> 9, of which waited for: 7 -> 6; matrix products, arithmetic and copies ran while one was open for 19% -> 16% of each run, Pallas kernels for 0% -> 0%
where the time goes in v2:
time: 750 us; the launch traced here: 743 us
  waiting for transfers between devices  486 us (65%)
  matrix products  91.5 us (12%)
  blocking collectives  66.3 us (9%)
  local copies, waits for them, and re-layouts  46.1 us (6%)
  other arithmetic  36.3 us (5%)
  between operations  15.8 us (2%)
    reduce_scatter x2, waiting for transfers between devices, scatter_cores(): lax.psum_scatter(array, BOTH, scatter_dimension=0, axis_index_groups=grou...  273 us
    all_gather x1, waiting for transfers between devices, local(): lax.all_gather(lax.dynamic_slice_in_dim(ffn_weight, (group * CHUNKS + c)...  154 us
    all_gather x1, waiting for transfers between devices, local(): lax.all_gather(lax.dynamic_slice_in_dim(attn_weight, group * attn_rows, a...  54.7 us
    psum x1, blocking collectives, local(): small = lax.psum(small, BOTH)  40.9 us
    dot_general x5, matrix products, times_trans(): lax.dot_general(left, right, (((1,), (1,)), ((), ())), preferred_element_...  27.7 us
    dot_general x8, matrix products, trans_times(): lax.dot_general(left, right, (((0,), (0,)), ((), ())), preferred_element_...  23 us
  transfers between devices with their start and end apart: 9, of which 6 were waited for; matrix products, arithmetic and copies ran while one was open for 16% of the time, Pallas kernels for 0%

profile of v2, /device:TPU:0, one launch (start us, length us, event | category | flops | bytes accessed | tf_op | source)
XLA Modules:
  0.0 743.3 jit_solution(15855588632876294455)
XLA Ops:
  11.0 13.5 %all-gather.2 = bf16[8,136,2]{1,2,0:T(2,128)(2,1)S(1)} all-gather(bf16[1,136,2]{1,2,0:T(2,128)(2,1)S(1)} %maximum_bitcast_fusion.3), channel_id=2, replica_groups=mesh['rep'=4,'shard'=8] {'shard'}, dimensions={0}, use_global_device_ids=true | all-gather | bytes 4896 | tf_op jit(solution)/shard_map/all_gather | solution.py:82
  29.0 54.7 %all-gather.11.cloned.1.call-done = bf16[1024,3072]{1,0:T(8,128)(2,1)} async-done(((bf16[32,3072]{1,0:T(8,128)(2,1)}), bf16[1024,3072]{1,0:T(8,128)(2,1)}) %all-gather.11.cloned.1.call-update) | async-done | bytes 6291472 | tf_op jit(solution)/shard_map/all_gather | solution.py:73
  83.6 3.3 copy.118
  101.3 153.8 %all-gather.7.cloned.1.call-done = bf16[4608,3,1024]{2,0,1:T(8,128)(2,1)} async-done(((bf16[144,3,1024]{2,0,1:T(8,128)(2,1)}), bf16[4608,3,1024]{2,0,1:T(8,128)(2,1)}) %all-gather.7.cloned.1.call-update) | async-done | bytes 28311568 | tf_op jit(solution)/shard_map/all_gather | solution.py:87
  255.1 5.4 fusion.1
  260.5 5.3 fusion.3
  265.8 8.8 %multiply_convert_fusion = (bf16[256,4608]{1,0:T(8,128)(2,1)}, bf16[256,4608]{1,0:T(8,128)(2,1)}, bf16[256,4608]{1,0:T(8,128)(2,1)}) fusion(f32[256,4608]{1,0:T(8,128)S(1)} %fusion.1, f32[256,4608]{1,0:T(8,128)S(1)} %fusion.3, bf16[4608,3,1024]{2,0,1:T(8,128)(2,1)} %all-gather.7.cloned.1.call-done, bf16[256,1024]{1,0:T(8,128)(2,1)S(1)} %copy-done.17, ...), kind=kOutput, calls=%fused_computation.23 | convolution fusion | flops 2434400256 | bytes 26477568 | tf_op jit(solution)/shard_map/dot_general | solution.py:41
  274.7 2.8 copy.144
  277.5 4.3 copy.143
  281.8 3.4 constant_dynamic-slice_fusion.3
  285.2 3.6 convolution_convert_fusion.1
  289.1 3.6 convolution_convert_fusion
  293.0 3.0 copy.142
  298.8 3.9 fusion.8
  303.8 3.8 fusion.9
  311.9 6.3 pad_maximum_fusion
  321.4 6.6 fusion
  328.1 6.3 multiply_reduce_fusion.1
  334.8 3.1 fusion.34
  339.2 4.0 fusion.37
  345.2 5.2 fusion.13
  367.8 3.4 convolution_convert_fusion.3
  371.2 2.8 pad_maximum_fusion.1
  377.3 3.1 copy.137
  380.6 5.6 fusion.44
  386.2 5.0 fusion.6
  391.2 145.3 %reduce-scatter.3.cloned.1.call-done = bf16[144,3,1024]{2,0,1:T(8,128)(2,1)} async-done(((bf16[2304,3,1024]{2,0,1:T(8,128)(2,1)}), bf16[144,3,1024]{2,0,1:T(8,128)(2,1)}) %reduce-scatter.3.cloned.1.call-update) | async-done | bytes 884752 | tf_op jit(solution)/shard_map/reduce_scatter | solution.py:58
  539.5 7.8 %fusion.33 = bf16[256,1024]{1,0:T(8,128)(2,1)} fusion(f32[256,1024]{1,0:T(8,128)S(1)} %copy-done.11, bf16[256,4608]{1,0:T(8,128)(2,1)} %get-tuple-element.18, bf16[4608,3,1024]{2,0,1:T(8,128)(2,1)} %all-gather.7.cloned.1.call-done, f32[256]{0:T(256)S(1)} %copy-done.44), kind=kOutput, calls=%fused_computation.58 | convolution fusion | flops 2416705536 | bytes 13370368 | tf_op jit(solution)/shard_map/dot_general | solution.py:177
  547.3 40.9 %psum.7 = f32[2,1088]{1,0:T(2,128)S(1)} all-reduce(f32[2,1088]{1,0:T(2,128)S(1)} %maximum_maximum_fusion), channel_id=1, replica_groups=mesh['rep'=4,'shard'=8] {'rep','shard'}, use_global_device_ids=true, to_apply=%region_19.20 | all-reduce | flops 2176 | bytes 17408 | tf_op jit(solution)/shard_map/psum | solution.py:255
  589.5 6.0 convert_element_type.220
  595.4 127.6 %reduce-scatter.5.cloned.1.call-done = bf16[32,3072]{1,0:T(8,128)(2,1)} async-done(((bf16[512,3072]{1,0:T(8,128)(2,1)}), bf16[32,3072]{1,0:T(8,128)(2,1)}) %reduce-scatter.5.cloned.1.call-update) | async-done | bytes 196624 | tf_op jit(solution)/shard_map/reduce_scatter | solution.py:58
  723.0 12.0 %all_gather.26 = bf16[128,3072]{1,0:T(8,128)(2,1)S(1)} all-gather(bf16[32,3072]{1,0:T(8,128)(2,1)} %reduce-scatter.5.cloned.1.call-done), channel_id=1, replica_groups=mesh['rep'=4,'shard'=8] {'rep'}, dimensions={0}, use_global_device_ids=true | all-gather | bytes 983040 | tf_op jit(solution)/shard_map/all_gather | solution.py:254
  (204 shorter events, 63.4 us)
Async XLA Ops:
  7.2 76.4 %all-gather.11.cloned.1.call-start = ((), (), s32[]{:S(2)}) async-start(), calls=%async_computation.6 | async-start | bytes 6488064 | tf_op jit(solution)/shard_map/all_gather | solution.py:73
  9.0 246.1 %all-gather.7.cloned.1.call-start = ((), (), s32[]{:S(2)}) async-start(), calls=%async_computation.2 | async-start | bytes 29196288 | tf_op jit(solution)/shard_map/all_gather | solution.py:87
  10.3 526.3 %reduce-scatter.3.cloned.1.call-start = ((), (), s32[]{:S(2)}) async-start(), calls=%async_computation.3 | async-start | bytes 15040512 | tf_op jit(solution)/shard_map/reduce_scatter | solution.py:58
  24.8 69.3 %copy-start.41 = (f32[64]{0:T(128)}, f32[64]{0:T(128)S(1)}, u32[]{:S(2)}) copy-start(f32[64]{0:T(128)S(1)} %reshape.301) | copy-start | bytes 772
  24.8 69.0 %copy-start.39 = (f32[64]{0:T(128)}, f32[64]{0:T(128)S(1)}, u32[]{:S(2)}) copy-start(f32[64]{0:T(128)S(1)} %reshape.300) | copy-start | bytes 772
  27.3 59.6 %copy-start.45 = (f32[256]{0:T(256)}, f32[256]{0:T(256)S(1)}, u32[]{:S(2)}) copy-start(f32[256]{0:T(256)S(1)} %add_rsqrt_fusion.3) | copy-start | bytes 3076
  83.6 6.0 copy-start.21
  101.3 159.2 %copy-start.6 = (bf16[256,1024]{1,0:T(8,128)(2,1)}, bf16[256,1024]{1,0:T(8,128)(2,1)S(1)}, u32[]{:S(2)}) copy-start(bf16[256,1024]{1,0:T(8,128)(2,1)S(1)} %multiply_convert_fusion.5) | copy-start | bytes 1572868
  260.5 5.3 copy-start.17
  260.5 5.3 copy-start.43
  288.8 9.9 %collective-permute-start.2 = (bf16[2304,1024]{1,0:T(8,128)(2,1)}, bf16[2304,1024]{1,0:T(8,128)(2,1)}, u32[]{:S(2)}, u32[]{:S(2)}) collective-permute-start(bf16[2304,1024]{1,0:T(8,128)(2,1)} %convolution_convert_fusion.1), channel_id=1, source_target_pairs={{0,1},{1,0},{2,3},{3,2},{4,5},{5,4},{6,7},{7,6},{8,9},{9,8},{10,11... | collective-permute-start | bytes 14155784 | tf_op jit(solution)/shard_map/ppermute | solution.py:53
  292.7 11.1 %collective-permute-start.3 = (bf16[2304,1024]{1,0:T(8,128)(2,1)}, bf16[2304,1024]{1,0:T(8,128)(2,1)}, u32[]{:S(2)}, u32[]{:S(2)}) collective-permute-start(bf16[2304,1024]{1,0:T(8,128)(2,1)} %convolution_convert_fusion), channel_id=1, source_target_pairs={{0,1},{1,0},{2,3},{3,2},{4,5},{5,4},{6,7},{7,6},{8,9},{9,8},{10,11... | collective-permute-start | bytes 14155784 | tf_op jit(solution)/shard_map/ppermute | solution.py:53
  298.4 12.0 %collective-permute-start.1 = (bf16[2304,1024]{1,0:T(8,128)(2,1)S(1)}, bf16[2304,1024]{1,0:T(8,128)(2,1)S(1)}, u32[]{:S(2)}, u32[]{:S(2)}) collective-permute-start(bf16[2304,1024]{1,0:T(8,128)(2,1)S(1)} %convolution_convert_fusion.2), channel_id=1, source_target_pairs={{0,1},{1,0},{2,3},{3,2},{4,5},{5,4},{6,7},{7,6},{8,9},{9,8},{10,11... | collective-permute-start | bytes 14155784 | tf_op jit(solution)/shard_map/ppermute | solution.py:53
  318.2 271.3 %all-gather.9.cloned.1.call-start = ((), (), s32[]{:S(2)}) async-start(), calls=%async_computation.5 | async-start | bytes 4423680 | tf_op jit(solution)/shard_map/all_gather | solution.py:251
  321.4 6.6 copy-start.10
  321.4 6.6 copy-start.14
  328.0 6.3 copy-start.20
  337.9 7.1 copy-start.16
  345.2 5.3 copy-start.27
  345.2 5.3 copy-start.29
  362.5 5.3 copy-start.22
  362.5 5.3 copy-start.38
  362.6 5.2 copy-start.46
  376.9 9.2 %collective-permute-start = (bf16[512,3072]{1,0:T(8,128)(2,1)}, bf16[512,3072]{1,0:T(8,128)(2,1)}, u32[]{:S(2)}, u32[]{:S(2)}) collective-permute-start(bf16[512,3072]{1,0:T(8,128)(2,1)} %bitcast.54), channel_id=1, source_target_pairs={{0,1},{1,0},{2,3},{3,2},{4,5},{5,4},{6,7},{7,6},{8,9},{9,8},{10,11... | collective-permute-start | bytes 9437192 | tf_op jit(solution)/shard_map/ppermute | solution.py:53
  380.5 5.7 slice-start
  380.5 5.6 copy-start.47
  380.6 5.6 slice-start.1
  391.2 146.0 %copy-start.23 = (bf16[256,1024]{1,0:T(8,128)(2,1)S(1)}, bf16[256,1024]{1,0:T(8,128)(2,1)}, u32[]{:S(2)}) copy-start(bf16[256,1024]{1,0:T(8,128)(2,1)} %param.8) | copy-start | bytes 1572868
  391.2 148.3 %copy-start.11 = (f32[256,1024]{1,0:T(8,128)S(1)}, f32[256,1024]{1,0:T(8,128)}, u32[]{:S(2)}) copy-start(f32[256,1024]{1,0:T(8,128)} %copy-done.9) | copy-start | bytes 3145732
  391.2 148.3 %copy-start.44 = (f32[256]{0:T(256)S(1)}, f32[256]{0:T(256)}, u32[]{:S(2)}) copy-start(f32[256]{0:T(256)} %compare_convert_fusion) | copy-start | bytes 3076
  536.5 186.5 %reduce-scatter.5.cloned.1.call-start = ((), (), s32[]{:S(2)}) async-start(), calls=%async_computation.4 | async-start | bytes 3342336 | tf_op jit(solution)/shard_map/reduce_scatter | solution.py:58
  589.4 146.8 %copy-start.1 = (bf16[576,3,1024]{2,0,1:T(8,128)(2,1)S(1)}, bf16[576,3,1024]{2,0,1:T(8,128)(2,1)}, u32[]{:S(2)}) copy-start(bf16[576,3,1024]{2,0,1:T(8,128)(2,1)} %param.13) | copy-start | bytes 10616836
  (27 other events, 65.8 us)
Sparse Core Ops, SparseCore 0:
  11.6 72.0 all-gather.10
  87.4 167.6 all-gather.6
  318.3 218.1 reduce-scatter.2
  538.2 47.5 all-gather.8
  590.6 132.3 reduce-scatter.4
